TPU v7x, 32 devices: a whole 2x2x4 slice. The times are simulated.
32 devices in a mesh: groups: 2 (over y), ctx: 4 (over z), mp: 4 (over x, core).
Axes of the slice: x: 2, y: 2, z: 4, core: 2. Of those that a mesh axis runs over, the one named last changes fastest.
Arguments:
- query: bfloat16 [4096, 8192], P(('groups', 'ctx'), 'mp'), parts along dimension 0, may hold values from -200 to 200
- span_keys: bfloat16 [4096, 1024], P(('groups', 'ctx'), 'mp'), parts along dimension 0, may hold values from -6 to 6
- span_values: bfloat16 [4096, 1024], P(('groups', 'ctx'), 'mp'), parts along dimension 0, may hold values from -6 to 6
- cache_keys: bfloat16 [8192, 1024], P(('groups', 'ctx'), 'mp'), parts along dimension 0, may hold values from -13 to 13
- stored_values: bfloat16 [8192, 1024], P(('groups', 'ctx'), 'mp'), parts along dimension 0, may hold values from -6 to 6
- selected: int32 [8, 8, 2], P(('groups', 'ctx'), 'mp'), parts along dimension 0, may hold values from 0 to 7, as said below
Outputs:
- attended: bfloat16 [4096, 8192], P(('groups', 'ctx'), 'mp'), parts along dimension 0
There are 2 independent parts, one for each index of `groups`. A program takes and returns all parts, laid end to end along the dimension named above; each array names one. Nothing has to cross between parts.
Inputs may be any that keep to these rules, and one draw needn't show every extreme that they name: `selected`: the two blocks chosen for a query block and key head lie in different ranges of 2 consecutive blocks, starting at multiples of 2.
All inputs are finite; a program needn't handle non-finite values.
Results may differ from a plain program's by a relative error of at most 0.0047.
Values may be sent and summed in bfloat16 or wider, within the bound.
No kernel may reach another device: no remote copies, remote signals or barrier semaphores. Data moves between devices by JAX's collectives and lax.ppermute only.
A program may use at most 64 MiB of HBM per device.

v0:
```python
import jax
import jax.numpy as jnp
from jax import lax
from jax.sharding import PartitionSpec as P

QUERY_HEADS = 64
KEY_VALUE_HEADS = 8
HEAD_DIMENSION = 128


def attend(query_group, all_keys, all_values, query_group_count):
    block_rows = query_group.shape[0]
    head_size = all_keys.shape[1]
    score_scale = head_size ** (-0.5)
    query_pos = jnp.arange(block_rows, dtype=jnp.int32)[:, None]
    key_pos = jnp.arange(all_keys.shape[0], dtype=jnp.int32)[None, :]
    visible = (key_pos >= block_rows) | (key_pos <= query_pos)
    results = []
    for member in range(query_group_count):
        query_head = query_group[:, member * head_size : (member + 1) * head_size]
        scores = jnp.dot(query_head, all_keys.T, preferred_element_type=jnp.float32) * score_scale
        scores = jnp.where(visible, scores, jnp.float32(-1e30))
        maxima = jnp.max(scores, axis=1, keepdims=True)
        exponent = jnp.exp(scores - maxima)
        denominator = jnp.sum(exponent, axis=1, keepdims=True)
        weights = (exponent / denominator).astype(jnp.bfloat16)
        results.append(
            jnp.dot(weights, all_values, preferred_element_type=jnp.float32).astype(jnp.bfloat16)
        )
    return jnp.concatenate(results, axis=1)


def per_device(query, span_keys, span_values, cache_keys, stored_values, selected):
    block_rows = query.shape[0]
    head_size = HEAD_DIMENSION
    kv_local = span_keys.shape[1] // head_size
    query_group_count = QUERY_HEADS // KEY_VALUE_HEADS
    wanted = selected[0]
    initial = jnp.zeros((kv_local, 2, block_rows, 2 * head_size), jnp.bfloat16)
    begin_row = jnp.int32(0)
    key_piece = lax.all_gather(cache_keys, "ctx", axis=0, tiled=True)
    value_piece = lax.all_gather(stored_values, "ctx", axis=0, tiled=True)
    piece_rows = key_piece.shape[0]
    updated = initial
    for collect_key_value_head in range(kv_local):
        for slot_index in range(2):
            first_row = wanted[collect_key_value_head, slot_index] * block_rows
            inside = (first_row >= begin_row) & (first_row < begin_row + piece_rows)
            offset = jnp.clip(first_row, 0, piece_rows - block_rows)
            key_tile = lax.dynamic_slice(
                key_piece,
                (offset, jnp.int32(collect_key_value_head * head_size)),
                (block_rows, head_size),
            )
            value_tile = lax.dynamic_slice(
                value_piece,
                (offset, jnp.int32(collect_key_value_head * head_size)),
                (block_rows, head_size),
            )
            tile_block = jnp.concatenate([key_tile, value_tile], axis=1)
            updated = updated.at[collect_key_value_head, slot_index].set(
                jnp.where(inside, tile_block, updated[collect_key_value_head, slot_index])
            )
    results = []
    for key_value_head in range(kv_local):
        query_group = query[
            :,
            key_value_head
            * query_group_count
            * head_size : (key_value_head + 1)
            * query_group_count
            * head_size,
        ]
        all_keys = jnp.concatenate(
            [
                span_keys[:, key_value_head * head_size : (key_value_head + 1) * head_size],
                updated[key_value_head, 0, :, :head_size],
                updated[key_value_head, 1, :, :head_size],
            ],
            axis=0,
        )
        all_values = jnp.concatenate(
            [
                span_values[:, key_value_head * head_size : (key_value_head + 1) * head_size],
                updated[key_value_head, 0, :, head_size:],
                updated[key_value_head, 1, :, head_size:],
            ],
            axis=0,
        )
        results.append(attend(query_group, all_keys, all_values, query_group_count))
    return jnp.concatenate(results, axis=1)


def solution(mesh):
    in_specs = (
        P(("groups", "ctx"), "mp"),
        P(("groups", "ctx"), "mp"),
        P(("groups", "ctx"), "mp"),
        P(("groups", "ctx"), "mp"),
        P(("groups", "ctx"), "mp"),
        P(("groups", "ctx"), "mp", None),
    )
    out_specs = P(("groups", "ctx"), "mp")
    return jax.shard_map(
        per_device, mesh=mesh, in_specs=in_specs, out_specs=out_specs, check_vma=False
    )
```

profile of v0, /device:TPU:0, one launch (start us, length us, event | category | flops | bytes accessed | tf_op | source)
XLA Modules:
  0.0 166.1 jit_solution(3036520839376949744)
XLA Ops:
  6.5 0.7 all-gather.5.cloned.1.call-update
  7.3 0.7 all-gather.3.cloned.1.call-update
  8.0 1.4 fusion.116
  12.1 0.6 fusion.117
  12.7 1.0 fusion.115
  13.7 1.0 fusion.114
  14.7 42.9 %all-gather.5.cloned.1.call-done = bf16[4096,256]{1,0:T(8,128)(2,1)} async-done(((bf16[1024,256]{1,0:T(8,128)(2,1)}), bf16[4096,256]{1,0:T(8,128)(2,1)}) %all-gather.5.cloned.1.call-update) | async-done | bytes 2097168 | tf_op jit(solution)/shard_map/all_gather | solution.py:42
  57.6 1.2 dynamic-slice_bitcast_fusion.2
  58.8 45.0 %all-gather.3.cloned.1.call-done = bf16[4096,256]{1,0:T(8,128)(2,1)} async-done(((bf16[1024,256]{1,0:T(8,128)(2,1)}), bf16[4096,256]{1,0:T(8,128)(2,1)}) %all-gather.3.cloned.1.call-update) | async-done | bytes 2097168 | tf_op jit(solution)/shard_map/all_gather | solution.py:41
  103.9 1.2 dynamic-slice_bitcast_fusion.3
  105.2 1.3 fusion.97
  106.5 0.8 slice_bitcast_fusion.5
  107.3 5.6 %fusion.118 = (f32[512]{0:T(512)}, f32[512,1536]{0,1:T(8,128)}) fusion(bf16[512,2048]{1,0:T(8,128)(2,1)} %param.14, bf16[512,128]{1,0:T(8,128)(2,1)S(1)} %get-tuple-element.65, bf16[512,128]{1,0:T(8,128)(2,1)S(1)} %get-tuple-element.66, bf16[512,128]{1,0:T(8,128)(2,1)S(1)} %get-tuple-element.74, pred[1536]{0:T(1024)(128)(4,1)S(1)} %iota_compare_fusion.1), kind=kOutput, calls=%fused_computation.192 | convolution fusion | flops 206437888 | bytes 3673600 | tf_op jit(solution)/shard_map/dot_general | solution.py:21
  112.9 1.2 fusion.119
  114.1 1.2 fusion.120
  115.2 1.2 fusion.121
  116.4 1.2 fusion.122
  117.6 1.2 fusion.123
  118.8 1.2 fusion.124
  120.0 0.6 fusion.125
  120.6 0.1 slice_select_fusion.1
  120.9 1.2 fusion.126
  122.1 1.2 fusion.127
  123.3 1.2 fusion.128
  124.5 1.2 fusion.129
  125.7 0.6 fusion.130
  126.3 0.6 fusion.131
  127.0 0.6 fusion.132
  127.6 1.3 fusion.133
  128.9 3.0 %fusion.33 = f32[512]{0:T(512)} fusion(f32[512,1536]{0,1:T(8,128)} %get-tuple-element.82, f32[512]{0:T(512)} %get-tuple-element.81), kind=kLoop, calls=%fused_computation.82 | loop fusion | flops 1572352 | bytes 3149824 | tf_op jit(solution)/shard_map/reduce_sum | solution.py:25
  131.9 1.8 %fusion.34 = f32[512]{0:T(512)} fusion(f32[512,1536]{0,1:T(8,128)S(1)} %get-tuple-element.84, f32[512]{0:T(512)} %get-tuple-element.83), kind=kLoop, calls=%fused_computation.83 | loop fusion | flops 1572352 | bytes 3149824 | tf_op jit(solution)/shard_map/reduce_sum | solution.py:25
  133.7 3.3 %fusion.81 = bf16[512,2048]{0,1:T(8,128)(2,1)} fusion(f32[512,1536]{0,1:T(8,128)} %get-tuple-element.82, f32[512]{0:T(512)} %fusion.33, f32[512]{0:T(512)} %get-tuple-element.81, bf16[512,128]{1,0:T(8,128)(2,1)S(1)} %copy-done.2, bf16[512,128]{1,0:T(8,128)(2,1)S(1)} %copy-done.1, bf16[512,128]{1,0:T(8,128)(2,1)S(1)} %get-tuple-element.68), kind=kOutput, calls=%fused_computation.130 | convolution fusion | flops 204931072 | bytes 3674112 | tf_op jit(solution)/shard_map/dot_general | solution.py:28
  137.0 1.3 fusion.82
  138.3 1.3 fusion.35
  139.6 0.3 copy-done
  139.9 0.9 fusion.83
  140.8 0.5 fusion.36
  141.3 0.7 fusion.84
  142.0 0.5 fusion.37
  142.5 0.7 fusion.85
  143.2 0.5 fusion.38
  143.8 0.7 fusion.86
  144.5 0.5 fusion.39
  145.0 0.7 fusion.87
  145.7 0.5 fusion.40
  146.2 0.7 fusion.88
  146.9 0.5 fusion.41
  147.4 0.2 copy-done.7
  147.5 0.5 fusion.42
  148.0 0.7 fusion.89
  148.8 0.7 fusion.90
  149.5 0.5 fusion.43
  150.0 0.7 fusion.91
  150.7 0.5 fusion.44
  151.2 0.7 fusion.92
  151.9 0.5 fusion.45
  152.4 0.7 fusion.93
  153.1 0.8 fusion.46
  153.8 0.7 fusion.94
  154.5 0.5 fusion.47
  155.0 0.7 fusion.95
  155.7 0.5 fusion.48
  156.2 0.7 fusion.96
  156.9 2.4 %copy.7 = bf16[512,2048]{1,0:T(8,128)(2,1)} copy(bf16[512,2048]{0,1:T(8,128)(2,1)S(1)} %fusion.96) | data formatting | bytes 4194304 | tf_op jit(solution)/shard_map/concatenate | solution.py:91
  (37 shorter events, 0.3 us)
Async XLA Ops:
  6.5 51.1 %all-gather.5.cloned.1.call-start = ((), (), s32[]{:S(2)}) async-start(), calls=%async_computation.1 | async-start | bytes 2621440 | tf_op jit(solution)/shard_map/all_gather | solution.py:42
  7.3 96.6 %all-gather.3.cloned.1.call-start = ((), (), s32[]{:S(2)}) async-start(), calls=%async_computation | async-start | bytes 2621440 | tf_op jit(solution)/shard_map/all_gather | solution.py:41
  12.1 114.9 %copy-start.14 = (pred[1536]{0:T(1024)(128)(4,1)}, pred[1536]{0:T(1024)(128)(4,1)S(1)}, u32[]{:S(2)}) copy-start(pred[1536]{0:T(1024)(128)(4,1)S(1)} %iota_compare_fusion.1) | copy-start | bytes 4612
  106.5 6.4 %copy-start.15 = (bf16[512,2048]{1,0:T(8,128)(2,1)S(1)}, bf16[512,2048]{1,0:T(8,128)(2,1)}, u32[]{:S(2)}) copy-start(bf16[512,2048]{1,0:T(8,128)(2,1)} %param.14) | copy-start | bytes 6291460
  128.9 4.8 %copy-start.1 = (bf16[512,128]{1,0:T(8,128)(2,1)S(1)}, bf16[512,128]{1,0:T(8,128)(2,1)}, u32[]{:S(2)}) copy-start(bf16[512,128]{1,0:T(8,128)(2,1)} %get-tuple-element.63) | copy-start | bytes 393220
  128.9 4.8 %copy-start.2 = (bf16[512,128]{1,0:T(8,128)(2,1)S(1)}, bf16[512,128]{1,0:T(8,128)(2,1)}, u32[]{:S(2)}) copy-start(bf16[512,128]{1,0:T(8,128)(2,1)} %get-tuple-element.64) | copy-start | bytes 393220
  133.7 3.3 %copy-start.12 = (f32[512]{0:T(512)S(1)}, f32[512]{0:T(512)}, u32[]{:S(2)}) copy-start(f32[512]{0:T(512)} %get-tuple-element.83) | copy-start | bytes 6148
  133.7 3.3 %copy-start.13 = (f32[512]{0:T(512)S(1)}, f32[512]{0:T(512)}, u32[]{:S(2)}) copy-start(f32[512]{0:T(512)} %fusion.34) | copy-start | bytes 6148
  138.3 1.6 copy-start
  138.3 1.6 copy-start.11
  139.9 0.9 copy-start.10
  141.3 0.7 copy-start.8
  142.5 0.7 copy-start.6
  143.7 0.7 copy-start.4
  146.2 0.7 copy-start.9
  146.9 0.7 copy-start.7
  148.7 0.7 copy-start.5
  150.0 0.7 copy-start.3
Sparse Core Ops, SparseCore 0:
  8.9 48.6 all-gather.4
  59.2 44.6 all-gather.2
where the time goes:
time: 167 us; the launch traced here: 166 us
  waiting for transfers between devices  89.3 us (53%)
  matrix products  35.8 us (21%)
  between operations  16.3 us (10%)
  other arithmetic  14.2 us (9%)
  local copies, waits for them, and re-layouts  10.4 us (6%)
    all_gather x1, waiting for transfers between devices, per_device(): key_piece = lax.all_gather(cache_keys, 'ctx', axis=0, tiled=True)  45 us
    all_gather x1, waiting for transfers between devices, per_device(): value_piece = lax.all_gather(stored_values, 'ctx', axis=0, tiled=True)  42.9 us
    dot_general x16, matrix products, attend(): jnp.dot(query_head, all_keys.T, preferred_element_type=jnp.float32)  21.3 us
    dot_general x16, matrix products, attend(): jnp.dot(weights, all_values, preferred_element_type=jnp.float32)  14.5 us
    reduce_sum x16, other arithmetic, attend(): denominator = jnp.sum(exponent, axis=1, keepdims=True)  12.8 us
  transfers between devices with their start and end apart: 2, of which 2 were waited for; matrix products, arithmetic and copies ran while one was open for 3% of the time, Pallas kernels for 0%

commit v1 on v0

--- a/solution.py
+++ b/solution.py
@@ -6,6 +6,16 @@
 QUERY_HEADS = 64
 KEY_VALUE_HEADS = 8
 HEAD_DIMENSION = 128
+
+
+def around_the_ring(x, axis, dim):
+    size = lax.axis_size(axis)
+    held, blocks = (x, [x])
+    for _ in range(size - 1):
+        held = lax.ppermute(held, axis, [(i, (i + 1) % size) for i in range(size)])
+        blocks.insert(0, held)
+    row_of_blocks = jnp.concatenate(blocks, axis=dim)
+    return jnp.roll(row_of_blocks, (lax.axis_index(axis) + 1) * x.shape[dim], axis=dim)
 
 
 def attend(query_group, all_keys, all_values, query_group_count):
@@ -38,7 +48,7 @@
     wanted = selected[0]
     initial = jnp.zeros((kv_local, 2, block_rows, 2 * head_size), jnp.bfloat16)
     begin_row = jnp.int32(0)
-    key_piece = lax.all_gather(cache_keys, "ctx", axis=0, tiled=True)
+    key_piece = around_the_ring(cache_keys, "ctx", 0)
     value_piece = lax.all_gather(stored_values, "ctx", axis=0, tiled=True)
     piece_rows = key_piece.shape[0]
     updated = initial

time: 167 us -> 144 us (0.86)
  waiting for transfers between devices: 89.3 us -> 52.4 us
  starting transfers between devices: 0.04 us -> 15.4 us
    ppermute x0 -> x3, waiting for transfers between devices: none -> 51.7 us  [around_the_ring(): held = lax.ppermute(held, axis, [(i, (i + 1) % size) for i in range(size)])]
    all_gather x1 -> x0, waiting for transfers between devices: 45 us -> none  [per_device(): key_piece = lax.all_gather(cache_keys, 'ctx', axis=0, tiled=True)]
    all_gather x1, waiting for transfers between devices: 42.9 us -> 0.02 us  [per_device(): value_piece = lax.all_gather(stored_values, 'ctx', axis=0, tiled=True)]
    ppermute x0 -> x3, starting transfers between devices: none -> 15.4 us  [around_the_ring(): held = lax.ppermute(held, axis, [(i, (i + 1) % size) for i in range(size)])]
  transfers between devices with their start and end apart: 2 -> 4, of which waited for: 2 -> 3; matrix products, arithmetic and copies ran while one was open for 3% -> 3% of each run, Pallas kernels for 0% -> 0%
where the time goes in v1:
time: 144 us
  waiting for transfers between devices  52.4 us (36%)
  matrix products  35.9 us (25%)
  between operations  16.3 us (11%)
  starting transfers between devices  15.4 us (11%)
  other arithmetic  14.2 us (10%)
  local copies, waits for them, and re-layouts  9.58 us (7%)
    ppermute x3, waiting for transfers between devices, around_the_ring(): held = lax.ppermute(held, axis, [(i, (i + 1) % size) for i in range(size)])  51.7 us
    dot_general x16, matrix products, attend(): jnp.dot(query_head, all_keys.T, preferred_element_type=jnp.float32)  21.3 us
    ppermute x3, starting transfers between devices, around_the_ring(): held = lax.ppermute(held, axis, [(i, (i + 1) % size) for i in range(size)])  15.4 us
    dot_general x16, matrix products, attend(): jnp.dot(weights, all_values, preferred_element_type=jnp.float32)  14.5 us
    reduce_sum x16, other arithmetic, attend(): denominator = jnp.sum(exponent, axis=1, keepdims=True)  12.7 us
  transfers between devices with their start and end apart: 4, of which 3 were waited for; matrix products, arithmetic and copies ran while one was open for 3% of the time, Pallas kernels for 0%

profile of v1, /device:TPU:0, one launch (start us, length us, event | category | flops | bytes accessed | tf_op | source)
XLA Modules:
  0.0 143.8 jit_solution(3926737834950121380)
XLA Ops:
  6.5 0.7 all-gather.2.cloned.1.call-update
  7.3 3.1 %collective-permute-start = (bf16[1024,256]{1,0:T(8,128)(2,1)}, bf16[1024,256]{1,0:T(8,128)(2,1)S(1)}, u32[]{:S(2)}, u32[]{:S(2)}) collective-permute-start(bf16[1024,256]{1,0:T(8,128)(2,1)} %param.17), channel_id=1, source_target_pairs={{0,4},{4,8},{8,12},{12,0},{1,5},{5,9},{9,13},{13,1},{2,6},{6,10},{... | collective-permute-start | bytes 1572872 | tf_op jit(solution)/shard_map/ppermute | solution.py:15
  10.3 15.3 %collective-permute-done = bf16[1024,256]{1,0:T(8,128)(2,1)S(1)} collective-permute-done((bf16[1024,256]{1,0:T(8,128)(2,1)}, bf16[1024,256]{1,0:T(8,128)(2,1)S(1)}, u32[]{:S(2)}, u32[]{:S(2)}) %collective-permute-start) | collective-permute-done | bytes 524320 | tf_op jit(solution)/shard_map/ppermute | solution.py:15
  25.7 3.0 %collective-permute-start.1 = (bf16[1024,256]{1,0:T(8,128)(2,1)S(1)}, bf16[1024,256]{1,0:T(8,128)(2,1)S(1)}, u32[]{:S(2)}, u32[]{:S(2)}) collective-permute-start(bf16[1024,256]{1,0:T(8,128)(2,1)S(1)} %collective-permute-done), channel_id=1, source_target_pairs={{0,4},{4,8},{8,12},{12,0},{1,5},{5,9},{9,13},{13,1},{2,6},{6,10},{... | collective-permute-start | bytes 1572872 | tf_op jit(solution)/shard_map/ppermute | solution.py:15
  28.7 1.4 %fusion.116 = (s32[1,1]{1,0:T(1,128)}, s32[1,1]{1,0:T(1,128)}, s32[1,1]{1,0:T(1,128)}, s32[1,1]{1,0:T(1,128)}) fusion(s32[2,2]{1,0:T(2,128)} %bitcast.107), kind=kLoop, calls=%fused_computation.198 | loop fusion | bytes 32 | tf_op jit(solution)/shard_map/slice | solution.py:57
  32.7 0.6 fusion.117
  33.3 21.7 %collective-permute-done.1 = bf16[1024,256]{1,0:T(8,128)(2,1)S(1)} collective-permute-done((bf16[1024,256]{1,0:T(8,128)(2,1)S(1)}, bf16[1024,256]{1,0:T(8,128)(2,1)S(1)}, u32[]{:S(2)}, u32[]{:S(2)}) %collective-permute-start.1) | collective-permute-done | bytes 524320 | tf_op jit(solution)/shard_map/ppermute | solution.py:15
  55.1 9.3 %collective-permute-start.2 = (bf16[1024,256]{1,0:T(8,128)(2,1)S(1)}, bf16[1024,256]{1,0:T(8,128)(2,1)S(1)}, u32[]{:S(2)}, u32[]{:S(2)}) collective-permute-start(bf16[1024,256]{1,0:T(8,128)(2,1)S(1)} %collective-permute-done.1), channel_id=1, source_target_pairs={{0,4},{4,8},{8,12},{12,0},{1,5},{5,9},{9,13},{13,1},{2,6},{6,10},{... | collective-permute-start | bytes 1572872 | tf_op jit(solution)/shard_map/ppermute | solution.py:15
  64.4 1.0 fusion.115
  65.4 1.0 fusion.114
  66.4 14.6 %collective-permute-done.2 = bf16[1024,256]{1,0:T(8,128)(2,1)S(1)} collective-permute-done((bf16[1024,256]{1,0:T(8,128)(2,1)S(1)}, bf16[1024,256]{1,0:T(8,128)(2,1)S(1)}, u32[]{:S(2)}, u32[]{:S(2)}) %collective-permute-start.2) | collective-permute-done | bytes 524320 | tf_op jit(solution)/shard_map/ppermute | solution.py:15
  81.5 1.3 dynamic-slice_bitcast_fusion.2
  82.9 1.3 fusion.97
  84.2 0.8 slice_bitcast_fusion.5
  85.0 5.6 %fusion.118 = (f32[512]{0:T(512)}, f32[512,1536]{0,1:T(8,128)}) fusion(bf16[512,2048]{1,0:T(8,128)(2,1)} %param.14, bf16[512,128]{1,0:T(8,128)(2,1)S(1)} %get-tuple-element.65, bf16[512,128]{1,0:T(8,128)(2,1)S(1)} %get-tuple-element.66, bf16[512,128]{1,0:T(8,128)(2,1)S(1)} %get-tuple-element.74, pred[1536]{0:T(1024)(128)(4,1)S(1)} %iota_compare_fusion.1), kind=kOutput, calls=%fused_computation.200 | convolution fusion | flops 206437888 | bytes 3673600 | tf_op jit(solution)/shard_map/dot_general | solution.py:31
  90.6 1.2 fusion.119
  91.7 1.2 fusion.120
  92.9 1.2 fusion.121
  94.1 1.2 fusion.122
  95.3 1.2 fusion.123
  96.5 1.2 fusion.124
  97.7 0.6 fusion.125
  98.6 1.2 fusion.126
  99.8 1.2 fusion.127
  101.0 1.2 fusion.128
  102.2 1.2 fusion.129
  103.4 0.6 fusion.130
  104.1 0.6 fusion.131
  104.7 0.6 fusion.132
  105.3 1.3 fusion.133
  106.6 3.0 %fusion.33 = f32[512]{0:T(512)} fusion(f32[512,1536]{0,1:T(8,128)} %get-tuple-element.82, f32[512]{0:T(512)} %get-tuple-element.81), kind=kLoop, calls=%fused_computation.82 | loop fusion | flops 1572352 | bytes 3149824 | tf_op jit(solution)/shard_map/reduce_sum | solution.py:35
  109.6 1.7 %fusion.34 = f32[512]{0:T(512)} fusion(f32[512,1536]{0,1:T(8,128)S(1)} %get-tuple-element.84, f32[512]{0:T(512)} %get-tuple-element.83), kind=kLoop, calls=%fused_computation.83 | loop fusion | flops 1572352 | bytes 3149824 | tf_op jit(solution)/shard_map/reduce_sum | solution.py:35
  111.3 3.3 %fusion.81 = bf16[512,2048]{0,1:T(8,128)(2,1)} fusion(f32[512,1536]{0,1:T(8,128)} %get-tuple-element.82, f32[512]{0:T(512)} %fusion.33, f32[512]{0:T(512)} %get-tuple-element.81, bf16[512,128]{1,0:T(8,128)(2,1)S(1)} %copy-done.3, bf16[512,128]{1,0:T(8,128)(2,1)S(1)} %copy-done.2, bf16[512,128]{1,0:T(8,128)(2,1)S(1)} %get-tuple-element.68), kind=kOutput, calls=%fused_computation.130 | convolution fusion | flops 204931072 | bytes 3674112 | tf_op jit(solution)/shard_map/dot_general | solution.py:38
  114.6 1.3 fusion.82
  115.9 1.3 fusion.35
  117.2 0.3 copy-done
  117.5 0.9 fusion.83
  118.4 0.5 fusion.36
  118.9 0.7 fusion.84
  119.6 0.5 fusion.37
  120.1 0.7 fusion.85
  120.9 0.5 fusion.38
  121.4 0.7 fusion.86
  122.1 0.5 fusion.39
  122.6 0.7 fusion.87
  123.3 0.5 fusion.40
  123.8 0.7 fusion.88
  124.5 0.5 fusion.41
  125.2 0.5 fusion.42
  125.7 0.7 fusion.89
  126.4 0.7 fusion.90
  127.1 0.5 fusion.43
  127.6 0.7 fusion.91
  128.3 0.5 fusion.44
  128.8 0.7 fusion.92
  129.5 0.5 fusion.45
  130.0 0.7 fusion.93
  130.7 0.8 fusion.46
  131.4 0.7 fusion.94
  132.1 0.5 fusion.47
  132.6 0.7 fusion.95
  133.3 0.5 fusion.48
  133.8 0.7 fusion.96
  134.5 2.4 %copy.7 = bf16[512,2048]{1,0:T(8,128)(2,1)} copy(bf16[512,2048]{0,1:T(8,128)(2,1)S(1)} %fusion.96) | data formatting | bytes 4194304 | tf_op jit(solution)/shard_map/concatenate | solution.py:101
  (50 shorter events, 1.1 us)
Async XLA Ops:
  6.5 74.5 %copy-start.1 = (bf16[1024,256]{1,0:T(8,128)(2,1)S(1)}, bf16[1024,256]{1,0:T(8,128)(2,1)}, u32[]{:S(2)}) copy-start(bf16[1024,256]{1,0:T(8,128)(2,1)} %param.17) | copy-start | bytes 1572868
  6.5 74.9 %all-gather.2.cloned.1.call-start = ((), (), s32[]{:S(2)}) async-start(), calls=%async_computation | async-start | bytes 2621440 | tf_op jit(solution)/shard_map/all_gather | solution.py:52
  7.3 18.4 %collective-permute-start = (bf16[1024,256]{1,0:T(8,128)(2,1)}, bf16[1024,256]{1,0:T(8,128)(2,1)S(1)}, u32[]{:S(2)}, u32[]{:S(2)}) collective-permute-start(bf16[1024,256]{1,0:T(8,128)(2,1)} %param.17), channel_id=1, source_target_pairs={{0,4},{4,8},{8,12},{12,0},{1,5},{5,9},{9,13},{13,1},{2,6},{6,10},{... | collective-permute-start | bytes 1572872 | tf_op jit(solution)/shard_map/ppermute | solution.py:15
  25.7 29.4 %collective-permute-start.1 = (bf16[1024,256]{1,0:T(8,128)(2,1)S(1)}, bf16[1024,256]{1,0:T(8,128)(2,1)S(1)}, u32[]{:S(2)}, u32[]{:S(2)}) collective-permute-start(bf16[1024,256]{1,0:T(8,128)(2,1)S(1)} %collective-permute-done), channel_id=1, source_target_pairs={{0,4},{4,8},{8,12},{12,0},{1,5},{5,9},{9,13},{13,1},{2,6},{6,10},{... | collective-permute-start | bytes 1572872 | tf_op jit(solution)/shard_map/ppermute | solution.py:15
  55.1 25.9 %collective-permute-start.2 = (bf16[1024,256]{1,0:T(8,128)(2,1)S(1)}, bf16[1024,256]{1,0:T(8,128)(2,1)S(1)}, u32[]{:S(2)}, u32[]{:S(2)}) collective-permute-start(bf16[1024,256]{1,0:T(8,128)(2,1)S(1)} %collective-permute-done.1), channel_id=1, source_target_pairs={{0,4},{4,8},{8,12},{12,0},{1,5},{5,9},{9,13},{13,1},{2,6},{6,10},{... | collective-permute-start | bytes 1572872 | tf_op jit(solution)/shard_map/ppermute | solution.py:15
  64.4 40.3 %copy-start.15 = (pred[1536]{0:T(1024)(128)(4,1)}, pred[1536]{0:T(1024)(128)(4,1)S(1)}, u32[]{:S(2)}) copy-start(pred[1536]{0:T(1024)(128)(4,1)S(1)} %iota_compare_fusion.1) | copy-start | bytes 4612
  84.2 6.4 %copy-start.16 = (bf16[512,2048]{1,0:T(8,128)(2,1)S(1)}, bf16[512,2048]{1,0:T(8,128)(2,1)}, u32[]{:S(2)}) copy-start(bf16[512,2048]{1,0:T(8,128)(2,1)} %param.14) | copy-start | bytes 6291460
  106.6 4.7 %copy-start.2 = (bf16[512,128]{1,0:T(8,128)(2,1)S(1)}, bf16[512,128]{1,0:T(8,128)(2,1)}, u32[]{:S(2)}) copy-start(bf16[512,128]{1,0:T(8,128)(2,1)} %get-tuple-element.63) | copy-start | bytes 393220
  106.6 4.7 %copy-start.3 = (bf16[512,128]{1,0:T(8,128)(2,1)S(1)}, bf16[512,128]{1,0:T(8,128)(2,1)}, u32[]{:S(2)}) copy-start(bf16[512,128]{1,0:T(8,128)(2,1)} %get-tuple-element.64) | copy-start | bytes 393220
  111.3 3.3 %copy-start.13 = (f32[512]{0:T(512)S(1)}, f32[512]{0:T(512)}, u32[]{:S(2)}) copy-start(f32[512]{0:T(512)} %get-tuple-element.83) | copy-start | bytes 6148
  111.3 3.3 %copy-start.14 = (f32[512]{0:T(512)S(1)}, f32[512]{0:T(512)}, u32[]{:S(2)}) copy-start(f32[512]{0:T(512)} %fusion.34) | copy-start | bytes 6148
  115.9 1.6 %copy-start = (bf16[512,2048]{0,1:T(8,128)(2,1)S(1)}, bf16[512,2048]{0,1:T(8,128)(2,1)}, u32[]{:S(2)}) copy-start(bf16[512,2048]{0,1:T(8,128)(2,1)} %fusion.82) | copy-start | bytes 6291460
  115.9 1.6 %copy-start.12 = (f32[512]{0:T(512)S(1)}, f32[512]{0:T(512)}, u32[]{:S(2)}) copy-start(f32[512]{0:T(512)} %get-tuple-element.85) | copy-start | bytes 6148
  117.5 0.9 copy-start.11
  118.9 0.7 copy-start.9
  120.1 0.7 copy-start.7
  121.4 0.7 copy-start.5
  123.8 0.7 copy-start.10
  124.5 0.7 copy-start.8
  126.4 0.7 copy-start.6
  127.6 0.7 copy-start.4
Sparse Core Ops, SparseCore 0:
  8.9 64.9 all-gather.1
